TPU v7x, 32 devices: a whole 2x2x4 slice. The times are simulated.
32 devices in a mesh: pop: 16 (over z, y, core), out: 2 (over x).
Axes of the slice: x: 2, y: 2, z: 4, core: 2. Of those that a mesh axis runs over, the one named last changes fastest.
Arguments:
- inputs: bfloat16 [6144, 4096], P(('pop', 'out')), may hold values from -6 to 6
- projection: bfloat16 [4096, 4096], P('pop', 'out'), may hold values from -0.09375 to 0.09375
- factor_a: bfloat16 [1536, 4096], P(('pop', 'out')), may hold values from -0.09375 to 0.09375
- factor_b: bfloat16 [1536, 4096], P('pop', 'out'), may hold values from -6 to 6
- fitness_w: float32 [1536], P('pop'), may hold values from -5 to 5
- elite_idx: int32 [384], P('pop'), may hold values from 0 to 95, as said below
Outputs:
- outputs: bfloat16 [6144, 4096], P('pop', 'out')
- update: float32 [4096, 4096], P('pop', 'out')
Inputs may be any that keep to these rules, and one draw needn't show every extreme that they name: `elite_idx`: the 24 entries of each aligned block of 24 are distinct members of that block's group.
All inputs are finite; a program needn't handle non-finite values.
Results may differ from a plain program's by a relative error of at most 0.0029.
Values may be sent and summed in bfloat16 or wider, within the bound.
A program may use at most 64 MiB of HBM per device.

v0:
```python
import math

import jax
import jax.numpy as jnp
from jax import lax
from jax.sharding import PartitionSpec as P


def outer_adder(scaled_all, shard_rows):
    return lax.dot_general(
        scaled_all, shard_rows, (((0,), (0,)), ((), ())), preferred_element_type=jnp.float32
    )


def shards(inputs, projection, factor_a, factor_b, fitness_w, elite_idx):
    whole_rows, whole_factor = (
        lax.all_gather(inputs, "out", axis=0, tiled=True),
        lax.all_gather(factor_a, "out", axis=0, tiled=True),
    )
    members = whole_factor.shape[0]
    per_member = whole_rows.shape[0] // members
    in_width = whole_factor.shape[1]
    grouped = whole_rows.reshape(members, per_member, in_width)
    member_dot = jnp.einsum(
        "mtd,md->mt", grouped, whole_factor, preferred_element_type=jnp.float32
    ).reshape(-1)
    projected = jnp.dot(
        whole_rows,
        lax.all_gather(projection, "pop", axis=0, tiled=True),
        preferred_element_type=jnp.float32,
    )
    spread_factor = jnp.repeat(factor_b.astype(jnp.float32), per_member, axis=0)
    outputs = (projected + member_dot[:, None] * spread_factor).astype(jnp.bfloat16)
    onehot = (elite_idx[:, None] == jnp.arange(members, dtype=jnp.int32)[None, :]).astype(
        jnp.float32
    )
    groups = lax.axis_size("pop")
    scale = math.sqrt(in_width / (groups * elite_idx.shape[0]))
    chosen_weight = jnp.dot(onehot, fitness_w, precision=lax.Precision.HIGHEST)
    chosen_factor = jnp.take(whole_factor, elite_idx, axis=0)
    scaled = (chosen_weight[:, None] * chosen_factor.astype(jnp.float32)).astype(jnp.bfloat16)
    scaled_all = lax.all_to_all(scaled, "pop", split_axis=1, concat_axis=0, tiled=True)
    chosen_cols = jnp.take(factor_b, elite_idx, axis=0)
    update_sum = outer_adder(scaled_all, lax.all_gather(chosen_cols, "pop", axis=0, tiled=True))
    return (outputs, update_sum * scale)


def solution(mesh):
    placed = (
        P(("pop", "out"), None),
        P("pop", "out"),
        P(("pop", "out"), None),
        P("pop", "out"),
        P("pop"),
        P("pop"),
    )
    return jax.shard_map(
        shards,
        mesh=mesh,
        in_specs=placed,
        out_specs=(P("pop", "out"), P("pop", "out")),
        check_vma=False,
    )
```

profile of v0, /device:TPU:0, one launch (start us, length us, event | category | flops | bytes accessed | tf_op | source)
XLA Modules:
  0.0 248.7 jit_solution(7622407939096387587)
XLA Ops:
  7.2 0.0 copy-start
  7.2 0.0 all-gather.8.cloned.1.call-start
  7.2 0.7 compare_select_fusion
  7.9 0.7 compare_and_fusion
  8.6 1.8 gather_fusion.1
  10.4 0.0 copy-start.5
  10.4 0.7 broadcast_select_fusion
  11.1 0.0 all-gather.8.cloned.1.call-update
  11.1 0.0 copy-start.3
  11.2 0.0 all-gather.4.cloned.1.call-start
  11.2 0.7 all-gather.4.cloned.1.call-update
  11.9 0.0 all-gather.6.cloned.1.call-start
  12.0 0.7 all-gather.6.cloned.1.call-update
  12.6 0.0 copy-done.4
  12.7 12.8 %all_gather.14 = bf16[96,4096]{1,0:T(8,128)(2,1)S(1)} all-gather(bf16[48,4096]{1,0:T(8,128)(2,1)S(1)} %copy-done.4), channel_id=1, replica_groups=mesh['pop'=16,'out'=2] {'out'}, dimensions={0}, use_global_device_ids=true | all-gather | bytes 1179648 | tf_op jit(solution)/shard_map/all_gather | solution.py:18
  25.4 0.7 gather_fusion
  26.1 0.2 convolution_bitcast_fusion
  26.3 0.8 multiply_convert_fusion
  27.1 0.0 copy-done.1
  27.1 6.2 %all-to-all-start = ((bf16[24,16,256]{2,0,1:T(8,128)(2,1)}), bf16[24,16,256]{2,0,1:T(8,128)(2,1)}, u32[]{:S(2)}, u32[]{:S(2)}) async-start(bf16[24,16,256]{2,0,1:T(8,128)(2,1)} %multiply_convert_fusion), calls=%async_computation | async-start | bytes 393216 | tf_op jit(solution)/shard_map/all_to_all | solution.py:42
  33.3 0.8 broadcast_in_dim.28
  34.2 2.8 %reshape.33 = f32[384,2048]{1,0:T(8,128)} reshape(f32[96,4,2048]{2,1,0:T(4,128)S(1)} %broadcast_in_dim.28) | data formatting | bytes 6291456 | tf_op jit(solution)/shard_map/reshape | solution.py:32
  36.9 5.4 %all-to-all-done = bf16[24,16,256]{2,0,1:T(8,128)(2,1)} async-done(((bf16[24,16,256]{2,0,1:T(8,128)(2,1)}), bf16[24,16,256]{2,0,1:T(8,128)(2,1)}, u32[]{:S(2)}, u32[]{:S(2)}) %all-to-all-start) | async-done | bytes 196640 | tf_op jit(solution)/shard_map/all_to_all | solution.py:42
  42.4 11.2 %all-gather.8.cloned.1.call-done = bf16[384,2048]{1,0:T(8,128)(2,1)} async-done(((bf16[24,2048]{1,0:T(8,128)(2,1)}), bf16[384,2048]{1,0:T(8,128)(2,1)}) %all-gather.8.cloned.1.call-update) | async-done | bytes 1572880 | tf_op jit(solution)/shard_map/all_gather | solution.py:44
  53.6 3.6 %convolution_multiply_fusion = f32[256,2048]{1,0:T(8,128)} fusion(bf16[384,256]{1,0:T(8,128)(2,1)} %bitcast.6, bf16[384,2048]{1,0:T(8,128)(2,1)} %all-gather.8.cloned.1.call-done), kind=kOutput, calls=%fused_computation.3 | convolution fusion | flops 403177472 | bytes 3866624 | tf_op jit(solution)/shard_map/dot_general | solution.py:10
  57.2 41.9 %all-gather.4.cloned.1.call-done = bf16[384,4096]{1,0:T(8,128)(2,1)} async-done(((bf16[192,4096]{1,0:T(8,128)(2,1)}), bf16[384,4096]{1,0:T(8,128)(2,1)}) %all-gather.4.cloned.1.call-update) | async-done | bytes 3145744 | tf_op jit(solution)/shard_map/all_gather | solution.py:17
  99.1 5.7 %reshape.32 = bf16[96,4,4096]{2,1,0:T(4,128)(2,1)} reshape(bf16[384,4096]{1,0:T(8,128)(2,1)} %all-gather.4.cloned.1.call-done) | data formatting | bytes 6291456 | tf_op jit(solution)/shard_map/reshape | solution.py:23
  104.8 0.0 copy-done.2
  104.8 6.0 %fusion = f32[96,1,4]{2,1,0:T(1,128)S(1)} fusion(bf16[96,4,4096]{2,1,0:T(4,128)(2,1)} %reshape.32, bf16[96,4096,1]{1,0,2:T(8,128)(2,1)S(1)} %bitcast.21), kind=kOutput, calls=%fused_computation.4 | convolution fusion | flops 3145728 | bytes 3933696 | tf_op jit(solution)/shard_map/mtd,md->mt/dot_general | solution.py:24
  110.8 0.1 mul.25
  111.0 116.7 %all-gather.6.cloned.1.call-done = bf16[4096,2048]{1,0:T(8,128)(2,1)} async-done(((bf16[256,2048]{1,0:T(8,128)(2,1)}), bf16[4096,2048]{1,0:T(8,128)(2,1)}) %all-gather.6.cloned.1.call-update) | async-done | bytes 16777232 | tf_op jit(solution)/shard_map/all_gather | solution.py:29
  227.7 14.5 %add_convert_fusion = bf16[384,2048]{1,0:T(8,128)(2,1)} fusion(f32[384,2048]{1,0:T(8,128)} %reshape.33, bf16[384,4096]{1,0:T(8,128)(2,1)} %all-gather.4.cloned.1.call-done, bf16[4096,2048]{1,0:T(8,128)(2,1)} %all-gather.6.cloned.1.call-done, f32[384]{0:T(512)S(1)} %mul.25), kind=kOutput, calls=%fused_computation.2 | convolution fusion | flops 6444810240 | bytes 24643072 | tf_op jit(solution)/shard_map/dot_general | solution.py:27
  (7 shorter events, 0.0 us)
Async XLA Ops:
  7.2 18.9 %copy-start = (f32[96]{0:T(128)S(1)}, f32[96]{0:T(128)}, u32[]{:S(2)}) copy-start(f32[96]{0:T(128)} %param.10) | copy-start | bytes 1156
  7.2 5.5 %copy-start.4 = (bf16[48,4096]{1,0:T(8,128)(2,1)S(1)}, bf16[48,4096]{1,0:T(8,128)(2,1)}, u32[]{:S(2)}) copy-start(bf16[48,4096]{1,0:T(8,128)(2,1)} %param.8) | copy-start | bytes 1179652
  7.2 46.4 %all-gather.8.cloned.1.call-start = ((), (), s32[]{:S(2)}) async-start(), calls=%async_computation.3 | async-start | bytes 1671168 | tf_op jit(solution)/shard_map/all_gather | solution.py:44
  10.4 15.7 %copy-start.5 = (s32[24]{0:T(128)S(1)}, s32[24]{0:T(128)}, u32[]{:S(2)}) copy-start(s32[24]{0:T(128)} %param.11) | copy-start | bytes 292
  11.1 22.2 %copy-start.3 = (bf16[96,2048]{1,0:T(8,128)(2,1)S(1)}, bf16[96,2048]{1,0:T(8,128)(2,1)}, u32[]{:S(2)}) copy-start(bf16[96,2048]{1,0:T(8,128)(2,1)} %param.9) | copy-start | bytes 1179652
  11.2 87.9 %all-gather.4.cloned.1.call-start = ((), (), s32[]{:S(2)}) async-start(), calls=%async_computation.1 | async-start | bytes 4718592 | tf_op jit(solution)/shard_map/all_gather | solution.py:17
  11.9 215.8 %all-gather.6.cloned.1.call-start = ((), (), s32[]{:S(2)}) async-start(), calls=%async_computation.2 | async-start | bytes 17825792 | tf_op jit(solution)/shard_map/all_gather | solution.py:29
  25.4 1.7 copy-start.1
  27.1 15.3 %all-to-all-start = ((bf16[24,16,256]{2,0,1:T(8,128)(2,1)}), bf16[24,16,256]{2,0,1:T(8,128)(2,1)}, u32[]{:S(2)}, u32[]{:S(2)}) async-start(bf16[24,16,256]{2,0,1:T(8,128)(2,1)} %multiply_convert_fusion), calls=%async_computation | async-start | bytes 393216 | tf_op jit(solution)/shard_map/all_to_all | solution.py:42
  57.1 47.6 %copy-start.2 = (bf16[96,4096]{1,0:T(8,128)(2,1)S(1)}, bf16[96,4096]{1,0:T(8,128)(2,1)}, u32[]{:S(2)}) copy-start(bf16[96,4096]{1,0:T(8,128)(2,1)} %copy-done.1) | copy-start | bytes 2359300
Sparse Core Ops, SparseCore 0:
  11.3 42.2 all-gather.7
  55.1 43.8 all-gather.3
  101.2 126.4 all-gather.5
where the time goes:
time: 249 us
  waiting for transfers between devices  177 us (71%)
  matrix products  24.3 us (10%)
  between operations  13.8 us (6%)
  blocking collectives  12.8 us (5%)
  local copies, waits for them, and re-layouts  11.9 us (5%)
  starting transfers between devices  6.34 us (3%)
  other arithmetic  2.9 us (1%)
    all_gather x1, waiting for transfers between devices, shards(): lax.all_gather(projection, 'pop', axis=0, tiled=True)  117 us
    all_gather x1, waiting for transfers between devices, shards(): lax.all_gather(inputs, 'out', axis=0, tiled=True)  41.9 us
    dot_general x1, matrix products, shards(): jnp.dot(whole_rows, lax.all_gather(projection, 'pop', axis=0, tiled=True)...  14.5 us
    all_gather x1, blocking collectives, shards(): lax.all_gather(factor_a, 'out', axis=0, tiled=True)  12.8 us
    all_gather x1, waiting for transfers between devices, shards(): lax.all_gather(chosen_cols, 'pop', axis=0, tiled=True)  11.2 us
    all_to_all x1, starting transfers between devices, shards(): lax.all_to_all(scaled, 'pop', split_axis=1, concat_axis=0, tiled=True)  6.22 us
    dot_general x1, matrix products, shards(): jnp.einsum('mtd,md->mt', grouped, whole_factor, preferred_element_type=jn...  6.05 us
    reshape x1, local copies, waits for them, and re-layouts, shards(): grouped = whole_rows.reshape(members, per_member, in_width)  5.72 us
  transfers between devices with their start and end apart: 4, of which 4 were waited for; matrix products, arithmetic and copies ran while one was open for 8% of the time, Pallas kernels for 0%

commit v1 on v0

v1 whole, which is shorter than its diff:
```python
import functools
import math

import jax
import jax.numpy as jnp
from jax import lax
from jax.experimental import pallas as pl
from jax.experimental.pallas import tpu as pltpu
from jax.sharding import PartitionSpec as P

MESH = pl.DeviceIdType.MESH
F32, BF16 = jnp.float32, jnp.bfloat16
CORES, Y = 2, 2


def chip_at(pos, n_chip):
    z_len = n_chip // Y
    y = pos // z_len
    z = pos * (1 - y) + (n_chip - 1 - pos) * y
    return z * Y + y


def kernel(
    n_pop, n_out, pieces, scale,
    x_ref, w_ref, a_ref, b_ref, f_ref, e_ref,
    out_ref, upd_ref,
    wbuf, bbuf, x_all, a_all, s_src, s_all, acc,
    ring_send, ring_recv, pair_send, pair_recv,
    xs_send, xs_recv, as_send, as_recv, s_send, s_recv, loc_sem,
):
    n_chip = n_pop // CORES
    z_len = n_chip // Y
    p, o = lax.axis_index("pop"), lax.axis_index("out")
    core, chip = p % CORES, p // CORES
    y, z = chip % Y, chip // Y
    pos = z * (1 - y) + (n_chip - 1 - z) * y
    kd, n_cols = w_ref.shape
    nh = n_cols // 2
    rows, d_in = x_ref.shape
    members = a_ref.shape[0]
    per_member = rows // members
    elite = e_ref.shape[0]
    depth = kd // pieces

    nxt = chip_at((pos + 1) % n_chip, n_chip) * CORES + core
    prv = chip_at((pos + n_chip - 1) % n_chip, n_chip) * CORES + core
    to = (nxt, prv)
    pair = chip * CORES + (1 - core)

    x_own = pltpu.make_async_copy(x_ref, x_all.at[o], loc_sem.at[0])
    a_own = pltpu.make_async_copy(a_ref, a_all.at[o], loc_sem.at[1])
    w_own = [
        pltpu.make_async_copy(
            w_ref.at[:, pl.ds(d * nh, nh)],
            wbuf.at[d, 0, pl.ds(pl.multiple_of(core * kd, kd), kd)],
            loc_sem.at[2 + d],
        )
        for d in range(2)
    ]
    for own in (a_own, x_own, *w_own):
        own.start()

    barrier = pltpu.get_barrier_semaphore()
    for k in range(1, n_pop):
        pl.semaphore_signal(
            barrier, inc=1, device_id={"pop": (p + k) % n_pop}, device_id_type=MESH
        )
    for k in range(1, n_out):
        pl.semaphore_signal(
            barrier, inc=1, device_id={"out": (o + k) % n_out}, device_id_type=MESH
        )
    pl.semaphore_wait(barrier, n_pop - 1 + n_out - 1)

    def piece(d, t, s, c):
        if s == pieces:
            return bbuf.at[d, t, c]
        return wbuf.at[
            d, t, pl.ds(pl.multiple_of(c * kd + s * depth, depth), depth)
        ]

    def source(d, t, s):
        if t == 0 and s < pieces:
            return w_ref.at[pl.ds(s * depth, depth), pl.ds(d * nh, nh)]
        return piece(d, t, s, core)

    def ring(d, t, s):
        return pltpu.make_async_remote_copy(
            src_ref=source(d, t, s),
            dst_ref=piece(d, t + 1, s, core),
            send_sem=ring_send.at[d, t, s],
            recv_sem=ring_recv.at[d, t, s],
            device_id={"pop": to[d]},
            device_id_type=MESH,
        )

    def across(d, t, s, c):
        return pltpu.make_async_remote_copy(
            src_ref=source(d, t, s) if c is core else piece(d, t, s, c),
            dst_ref=piece(d, t, s, c),
            send_sem=pair_send.at[d, t, s],
            recv_sem=pair_recv.at[d, t, s],
            device_id={"pop": pair},
            device_id_type=MESH,
        )

    def shared(k, src, dst, send, recv):
        return pltpu.make_async_remote_copy(
            src_ref=src,
            dst_ref=dst,
            send_sem=send.at[k],
            recv_sem=recv.at[k],
            device_id={"out": (o + k) % n_out},
            device_id_type=MESH,
        )

    def block_to(k):
        return pltpu.make_async_remote_copy(
            src_ref=s_src.at[(p + k) % n_pop],
            dst_ref=s_all.at[p],
            send_sem=s_send.at[k],
            recv_sem=s_recv.at[k],
            device_id={"pop": (p + k) % n_pop},
            device_id_type=MESH,
        )

    order = [0, pieces, *range(1, pieces)]
    for s in range(pieces):
        for d in range(2):
            ring(d, 0, s).start()
            across(d, 0, s, core).start()
        if s == 0:
            for k in range(1, n_out):
                shared(k, a_ref, a_all.at[o], as_send, as_recv).start()
            for k in range(1, n_out):
                shared(k, x_ref, x_all.at[o], xs_send, xs_recv).start()
            ids = e_ref[...]

            def picks(m):
                at = lax.broadcasted_iota(jnp.int32, (elite, members), 1) + m * members
                return (at == ids).astype(F32).astype(BF16)

            for d in range(2):
                total = jnp.zeros((elite, nh), F32)
                for m in range(n_out):
                    total += jnp.dot(
                        picks(m), b_ref[m, :, d * nh : (d + 1) * nh],
                        preferred_element_type=F32,
                    )
                bbuf[d, 0, core] = total.astype(BF16)
            upd_ref[...] = jnp.zeros_like(upd_ref)
    for d in range(2):
        ring(d, 0, pieces).start()
        across(d, 0, pieces, core).start()

    a_own.wait()
    for k in range(1, n_out):
        shared(k, a_ref, a_all.at[o], as_send, as_recv).wait_recv()
    every = lax.broadcasted_iota(jnp.int32, (elite, n_out * members), 1)
    weight = jnp.sum(jnp.where(every == ids, f_ref[...], 0.0), axis=1, keepdims=True)
    for q in range(n_pop):
        block = jnp.zeros((elite, kd), F32)
        for m in range(n_out):
            block += jnp.dot(
                picks(m), a_all[m, :, q * kd : (q + 1) * kd],
                preferred_element_type=F32,
            )
        s_src[q] = (weight * block).astype(BF16)
    s_all[p] = s_src[p]
    for k in range(1, n_pop):
        block_to(k).start()

    for own in w_own:
        own.wait()

    def chip_of(d, t):
        return chip_at((pos + (n_chip - t if d == 0 else t)) % n_chip, n_chip)

    tile = min(nh, 512)

    def project(d, t):
        off = pl.multiple_of(chip_of(d, t) * (CORES * kd), CORES * kd)
        x_part = x_all[:, :, pl.ds(off, CORES * kd)].reshape(n_out * rows, CORES * kd)
        for j in range(nh // tile):
            lo = d * nh + j * tile
            acc[:, lo : lo + tile] += jnp.dot(
                x_part, wbuf[d, t, :, j * tile : (j + 1) * tile],
                preferred_element_type=F32,
            )

    def update(d, t):
        for c in range(CORES):
            upd_ref[:, d * nh : (d + 1) * nh] += lax.dot_general(
                s_all[chip_of(d, t) * CORES + c], bbuf[d, t, c],
                (((0,), (0,)), ((), ())), preferred_element_type=F32,
            )

    def start_rows():
        x_own.wait()
        for k in range(1, n_out):
            shared(k, x_ref, x_all.at[o], xs_send, xs_recv).wait_recv()
        row = lax.broadcasted_iota(jnp.int32, (rows, members), 0) // per_member
        own = row == lax.broadcasted_iota(jnp.int32, (rows, members), 1)
        for m in range(n_out):
            dots = lax.dot_general(
                x_all[m], a_all[m], (((1,), (1,)), ((), ())),
                preferred_element_type=F32,
            )
            dots = jnp.where(own, dots, 0.0)
            high = dots.astype(BF16)
            rest = dots - high.astype(F32)
            mid = rest.astype(BF16)
            low = (rest - mid.astype(F32)).astype(BF16)
            for d in range(2):
                cols = slice(d * nh, (d + 1) * nh)
                b_part = b_ref[m, :, cols]
                acc[m * rows : (m + 1) * rows, cols] = (
                    jnp.dot(high, b_part, preferred_element_type=F32)
                    + jnp.dot(mid, b_part, preferred_element_type=F32)
                    + jnp.dot(low, b_part, preferred_element_type=F32)
                )

    def start_update():
        for k in range(1, n_pop):
            block_to(k).wait_recv()

    todo = []
    ready = max(1, n_chip // 2)
    for t in range(n_chip):
        if t == ready:
            todo = [start_rows, start_update] + todo
        for s in order:
            for d in range(2):
                if t:
                    ring(d, t - 1, s).wait_recv()
                    if t < n_chip - 1:
                        ring(d, t, s).start()
                    across(d, t, s, core).start()
            if t >= ready and t < n_chip - 1:
                for _ in range(min(3, len(todo))):
                    todo.pop(0)()
        for s in order:
            for d in range(2):
                across(d, t, s, 1 - core).wait_recv()
        for d in range(2):
            todo.append(functools.partial(update, d, t))
            todo.append(functools.partial(project, d, t))
    for job in todo:
        job()

    upd_ref[...] = upd_ref[...] * scale
    out_ref[...] = acc[...].astype(BF16)

    for t in range(n_chip):
        for s in order:
            for d in range(2):
                if t < n_chip - 1:
                    ring(d, t, s).wait_send()
                across(d, t, s, core).wait_send()
    for k in range(1, n_out):
        shared(k, a_ref, a_all.at[o], as_send, as_recv).wait_send()
        shared(k, x_ref, x_all.at[o], xs_send, xs_recv).wait_send()
    for k in range(1, n_pop):
        block_to(k).wait_send()


def solution(mesh):
    n_pop, n_out = mesh.shape["pop"], mesh.shape["out"]
    n_chip = n_pop // CORES

    def step(inputs, projection, factor_a, factor_b, fitness_w, elite_idx):
        rows, d_in = inputs.shape
        kd, n_cols = projection.shape
        members, elite = factor_a.shape[0], elite_idx.shape[0]
        nh = n_cols // 2
        pieces = min(4, kd // 16)
        scale = math.sqrt(d_in / (n_pop * elite))
        dma = pltpu.SemaphoreType.DMA
        hbm, vmem = pl.BlockSpec(memory_space=pl.ANY), pl.BlockSpec(memory_space=pltpu.VMEM)
        return pl.pallas_call(
            functools.partial(kernel, n_pop, n_out, pieces, scale),
            out_shape=(
                jax.ShapeDtypeStruct((n_out * rows, n_cols), BF16),
                jax.ShapeDtypeStruct((kd, n_cols), F32),
            ),
            in_specs=[hbm, hbm, hbm, vmem, vmem, vmem],
            out_specs=(vmem, vmem),
            scratch_shapes=[
                pltpu.VMEM((2, n_chip, CORES * kd, nh), BF16),
                pltpu.VMEM((2, n_chip, CORES, elite, nh), BF16),
                pltpu.VMEM((n_out, rows, d_in), BF16),
                pltpu.VMEM((n_out, members, d_in), BF16),
                pltpu.VMEM((n_pop, elite, kd), BF16),
                pltpu.VMEM((n_pop, elite, kd), BF16),
                pltpu.VMEM((n_out * rows, n_cols), F32),
                dma((2, n_chip, pieces + 1)),
                dma((2, n_chip, pieces + 1)),
                dma((2, n_chip, pieces + 1)),
                dma((2, n_chip, pieces + 1)),
                dma((n_out,)),
                dma((n_out,)),
                dma((n_out,)),
                dma((n_out,)),
                dma((n_pop,)),
                dma((n_pop,)),
                dma((4,)),
            ],
            compiler_params=pltpu.CompilerParams(
                collective_id=0, has_side_effects=True, vmem_limit_bytes=60 * 2**20
            ),
        )(
            inputs,
            projection,
            factor_a,
            factor_b.reshape(n_out, members, n_cols),
            fitness_w.reshape(1, -1),
            elite_idx.reshape(-1, 1),
        )

    return jax.shard_map(
        step,
        mesh=mesh,
        in_specs=(
            P(("pop", "out"), None),
            P("pop", "out"),
            P(("pop", "out"), None),
            P("pop", "out"),
            P("pop"),
            P("pop"),
        ),
        out_specs=(P("pop", "out"), P("pop", "out")),
        check_vma=False,
    )
```

time: 249 us -> 114 us (0.46)
  waiting for transfers between devices: 177 us -> 0 us
  Pallas kernels: 0 us -> 108 us
  matrix products: 24.3 us -> 0 us
  between operations: 13.8 us -> 0.65 us
  blocking collectives: 12.8 us -> 0 us
  local copies, waits for them, and re-layouts: 11.9 us -> 5.53 us
  starting transfers between devices: 6.34 us -> 0 us
  other arithmetic: 2.9 us -> 0 us
    all_gather x3 -> x0, waiting for transfers between devices: 170 us -> none  [the longest x1 117 us: shards(): lax.all_gather(projection, 'pop', axis=0, tiled=True)]
    pallas_call x0 -> x1, Pallas kernels: none -> 108 us  [step(): pl.pallas_call(functools.partial(kernel, n_pop, n_out, pieces, scale), ou...]
    dot_general x4 -> x0, matrix products: 24.3 us -> none  [the longest x1 14.5 us: shards(): jnp.dot(whole_rows, lax.all_gather(projection, 'pop', axis=0, tiled=True)...]
    all_gather x1 -> x0, blocking collectives: 12.8 us -> none  [shards(): lax.all_gather(factor_a, 'out', axis=0, tiled=True)]
    reshape x2 -> x1, local copies, waits for them, and re-layouts: 8.48 us -> 1.33 us  [step(): elite_idx.reshape(-1, 1)]
    all_to_all x1 -> x0, starting transfers between devices: 6.22 us -> none  [shards(): lax.all_to_all(scaled, 'pop', split_axis=1, concat_axis=0, tiled=True)]
    all_to_all x1 -> x0, waiting for transfers between devices: 5.41 us -> none  [shards(): lax.all_to_all(scaled, 'pop', split_axis=1, concat_axis=0, tiled=True)]
    unnamed x12 -> x4, local copies, waits for them, and re-layouts: 0.03 us -> 4.2 us
  transfers between devices with their start and end apart: 4 -> 0, of which waited for: 4 -> 0; matrix products, arithmetic and copies ran while one was open for 8% -> 0% of each run, Pallas kernels for 0% -> 0%
where the time goes in v1:
time: 114 us
  Pallas kernels  108 us (95%)
  local copies, waits for them, and re-layouts  5.53 us (5%)
    pallas_call x1, Pallas kernels, step(): pl.pallas_call(functools.partial(kernel, n_pop, n_out, pieces, scale), ou...  108 us
    unnamed x4, local copies, waits for them, and re-layouts  4.2 us

profile of v1, /device:TPU:0, one launch (start us, length us, event | category | flops | bytes accessed | tf_op | source)
XLA Modules:
  0.0 113.8 jit_solution(4317224306218240148)
XLA Ops:
  0.6 1.3 %copy.8.e_ref = s32[24,1]{1,0:T(8,128)} copy(s32[24,1]{0,1:T(1,128)} %bitcast.5) | data formatting | bytes 192 | tf_op jit(solution)/shard_map/reshape | solution.py:316
  2.0 107.6 %shard_map.77 = (bf16[384,2048]{1,0:T(8,128)(2,1)}, f32[256,2048]{1,0:T(8,128)}) custom-call(bf16[192,4096]{1,0:T(8,128)(2,1)} %x_ref.1, bf16[256,2048]{1,0:T(8,128)(2,1)} %w_ref.1, bf16[48,4096]{1,0:T(8,128)(2,1)} %a_ref.1, bf16[2,48,2048]{2,1,0:T(8,128)(2,1)} %bitcast.3, f32[1,96]{1,0:T(1,128)} %bitcast.4, s32[24,1]{1,0:T(8,128)} %copy.8.e_ref), custom_call_target="tpu_custom_call" | custom-call | tf_op jit(solution)/shard_map/pallas_call | solution.py:279
  109.6 0.0 copy-start
  109.6 2.9 %copy.11 = bf16[384,2048]{1,0:T(8,128)(2,1)} copy(bf16[384,2048]{1,0:T(8,128)(2,1)} %get-tuple-element.4) | data formatting | bytes 3145728
  112.5 0.0 copy-done
  112.5 1.3 %copy.12 = f32[256,2048]{1,0:T(8,128)} copy(f32[256,2048]{1,0:T(8,128)S(1)} %copy-done) | data formatting | bytes 4194304
Async XLA Ops:
  109.6 2.9 %copy-start = (f32[256,2048]{1,0:T(8,128)S(1)}, f32[256,2048]{1,0:T(8,128)}, u32[]{:S(2)}) copy-start(f32[256,2048]{1,0:T(8,128)} %get-tuple-element.5) | copy-start | bytes 6291460

commit v2 on v1

--- a/solution.py
+++ b/solution.py
@@ -21,10 +21,10 @@
 
 
 def kernel(
-    n_pop, n_out, pieces, scale,
-    x_ref, w_ref, a_ref, b_ref, f_ref, e_ref,
-    out_ref, upd_ref,
-    wbuf, bbuf, x_all, a_all, s_src, s_all, acc,
+    n_pop, n_out, pieces,
+    x_ref, w_ref, a_ref, b_hbm, f_hbm, e_hbm,
+    acc, upd_ref,
+    wbuf, bbuf, x_all, a_all, s_src, s_all, b_ref, f_ref, e_ref,
     ring_send, ring_recv, pair_send, pair_recv,
     xs_send, xs_recv, as_send, as_recv, s_send, s_recv, loc_sem,
 ):
@@ -39,7 +39,7 @@
     rows, d_in = x_ref.shape
     members = a_ref.shape[0]
     per_member = rows // members
-    elite = e_ref.shape[0]
+    elite = e_ref.shape[1]
     depth = kd // pieces
 
     nxt = chip_at((pos + 1) % n_chip, n_chip) * CORES + core
@@ -57,7 +57,11 @@
         )
         for d in range(2)
     ]
-    for own in (a_own, x_own, *w_own):
+    small = [
+        pltpu.make_async_copy(src, dst, loc_sem.at[4 + k])
+        for k, (src, dst) in enumerate(((e_hbm, e_ref), (b_hbm, b_ref), (f_hbm, f_ref)))
+    ]
+    for own in (*small, a_own, x_own, *w_own):
         own.start()
 
     barrier = pltpu.get_barrier_semaphore()
@@ -133,7 +137,13 @@
                 shared(k, a_ref, a_all.at[o], as_send, as_recv).start()
             for k in range(1, n_out):
                 shared(k, x_ref, x_all.at[o], xs_send, xs_recv).start()
-            ids = e_ref[...]
+            for own in small:
+                own.wait()
+            turned = lax.broadcasted_iota(jnp.int32, (elite, elite), 0)
+            turned = turned == lax.broadcasted_iota(jnp.int32, (elite, elite), 1)
+            ids = jnp.sum(
+                jnp.where(turned, e_ref[...].astype(F32), 0.0), axis=1, keepdims=True
+            ).astype(jnp.int32)
 
             def picks(m):
                 at = lax.broadcasted_iota(jnp.int32, (elite, members), 1) + m * members
@@ -247,8 +257,6 @@
     for job in todo:
         job()
 
-    upd_ref[...] = upd_ref[...] * scale
-    out_ref[...] = acc[...].astype(BF16)
 
     for t in range(n_chip):
         for s in order:
@@ -275,14 +283,14 @@
         pieces = min(4, kd // 16)
         scale = math.sqrt(d_in / (n_pop * elite))
         dma = pltpu.SemaphoreType.DMA
-        hbm, vmem = pl.BlockSpec(memory_space=pl.ANY), pl.BlockSpec(memory_space=pltpu.VMEM)
-        return pl.pallas_call(
-            functools.partial(kernel, n_pop, n_out, pieces, scale),
+        hbm, vmem = pl.BlockSpec(memory_space=pltpu.HBM), pl.BlockSpec(memory_space=pltpu.VMEM)
+        total, update_sum = pl.pallas_call(
+            functools.partial(kernel, n_pop, n_out, pieces),
             out_shape=(
-                jax.ShapeDtypeStruct((n_out * rows, n_cols), BF16),
+                jax.ShapeDtypeStruct((n_out * rows, n_cols), F32),
                 jax.ShapeDtypeStruct((kd, n_cols), F32),
             ),
-            in_specs=[hbm, hbm, hbm, vmem, vmem, vmem],
+            in_specs=[hbm] * 6,
             out_specs=(vmem, vmem),
             scratch_shapes=[
                 pltpu.VMEM((2, n_chip, CORES * kd, nh), BF16),
@@ -291,7 +299,9 @@
                 pltpu.VMEM((n_out, members, d_in), BF16),
                 pltpu.VMEM((n_pop, elite, kd), BF16),
                 pltpu.VMEM((n_pop, elite, kd), BF16),
-                pltpu.VMEM((n_out * rows, n_cols), F32),
+                pltpu.VMEM((n_out, members, n_cols), BF16),
+                pltpu.VMEM((1, n_out * members), F32),
+                pltpu.VMEM((1, elite), jnp.int32),
                 dma((2, n_chip, pieces + 1)),
                 dma((2, n_chip, pieces + 1)),
                 dma((2, n_chip, pieces + 1)),
@@ -302,10 +312,10 @@
                 dma((n_out,)),
                 dma((n_pop,)),
                 dma((n_pop,)),
-                dma((4,)),
+                dma((7,)),
             ],
             compiler_params=pltpu.CompilerParams(
-                collective_id=0, has_side_effects=True, vmem_limit_bytes=60 * 2**20
+                collective_id=0, has_side_effects=True, vmem_limit_bytes=44 * 2**20
             ),
         )(
             inputs,
@@ -313,8 +323,9 @@
             factor_a,
             factor_b.reshape(n_out, members, n_cols),
             fitness_w.reshape(1, -1),
-            elite_idx.reshape(-1, 1),
-        )
+            elite_idx.reshape(1, -1),
+        )
+        return total.astype(BF16), update_sum * scale
 
     return jax.shard_map(
         step,

time: 114 us -> 115 us (level)
  Pallas kernels: 108 us -> 104 us
  other arithmetic: 0 us -> 2.87 us
    pallas_call x1, Pallas kernels: 108 us -> 104 us  [step(): pl.pallas_call(functools.partial(kernel, n_pop, n_out, pieces), out_shape...]
    unnamed x4 -> x12, local copies, waits for them, and re-layouts: 4.2 us -> 5.93 us
    mul x0 -> x1, other arithmetic: none -> 1.5 us  [step(): return (total.astype(BF16), update_sum * scale)]
    convert_element_type x0 -> x1, other arithmetic: none -> 1.36 us  [step(): return (total.astype(BF16), update_sum * scale)]
    reshape x1 -> x0, local copies, waits for them, and re-layouts: 1.33 us -> none  [step(): elite_idx.reshape(-1, 1)]
where the time goes in v2:
time: 115 us; the launch traced here: 114 us
  Pallas kernels  104 us (90%)
  local copies, waits for them, and re-layouts  5.93 us (5%)
  other arithmetic  2.87 us (2%)
    pallas_call x1, Pallas kernels, step(): pl.pallas_call(functools.partial(kernel, n_pop, n_out, pieces), out_shape...  104 us
    unnamed x12, local copies, waits for them, and re-layouts  5.93 us

profile of v2, /device:TPU:0, one launch (start us, length us, event | category | flops | bytes accessed | tf_op | source)
XLA Modules:
  0.0 113.9 jit_solution(28308095838756800)
XLA Ops:
  0.6 0.0 copy-start
  0.6 1.4 %copy-done = bf16[192,4096]{1,0:T(8,128)(2,1)S(1)} copy-done((bf16[192,4096]{1,0:T(8,128)(2,1)S(1)}, bf16[192,4096]{1,0:T(8,128)(2,1)}, u32[]{:S(2)}) %copy-start) | copy-done | bytes 1572888
  2.0 0.0 copy-start.1
  2.0 1.2 %copy-done.1 = bf16[256,2048]{1,0:T(8,128)(2,1)S(1)} copy-done((bf16[256,2048]{1,0:T(8,128)(2,1)S(1)}, bf16[256,2048]{1,0:T(8,128)(2,1)}, u32[]{:S(2)}) %copy-start.1) | copy-done | bytes 1048600
  3.3 0.0 copy-start.2
  3.3 1.0 copy-done.2
  4.3 0.0 copy-start.3
  4.3 1.0 copy-done.3
  5.3 0.0 copy-start.4
  5.3 0.7 copy-done.4
  5.9 0.0 copy-start.5
  5.9 0.7 copy-done.5
  6.6 104.5 %shard_map.77 = (f32[384,2048]{1,0:T(8,128)S(1)}, f32[256,2048]{1,0:T(8,128)S(1)}) custom-call(bf16[192,4096]{1,0:T(8,128)(2,1)S(1)} %copy-done, bf16[256,2048]{1,0:T(8,128)(2,1)S(1)} %copy-done.1, bf16[48,4096]{1,0:T(8,128)(2,1)S(1)} %copy-done.2, bf16[2,48,2048]{2,1,0:T(8,128)(2,1)S(1)} %bitcast.3, f32[1,96]{1,0:T(1,128)S(1)} %bitcast.4, s32[1,24]{1,0:T(1,128)S(1)} %bitcast.5), custom_call_target="tpu_custom_call" | custom-call | tf_op jit(solution)/shard_map/pallas_call | solution.py:287
  111.1 1.4 %convert_element_type.3 = bf16[384,2048]{1,0:T(8,128)(2,1)} convert(f32[384,2048]{1,0:T(8,128)S(1)} %get-tuple-element.4) | non-fusion elementwise | flops 786432 | bytes 4718592 | tf_op jit(solution)/shard_map/convert_element_type | solution.py:328
  112.4 1.5 %broadcast_multiply_fusion = f32[256,2048]{1,0:T(8,128)} fusion(f32[256,2048]{1,0:T(8,128)S(1)} %get-tuple-element.5), kind=kLoop, calls=%fused_computation | loop fusion | flops 524288 | bytes 4194304 | tf_op jit(solution)/shard_map/mul | solution.py:328
Async XLA Ops:
  0.6 1.4 %copy-start = (bf16[192,4096]{1,0:T(8,128)(2,1)S(1)}, bf16[192,4096]{1,0:T(8,128)(2,1)}, u32[]{:S(2)}) copy-start(bf16[192,4096]{1,0:T(8,128)(2,1)} %x_ref.1) | copy-start | bytes 4718596
  2.0 1.2 %copy-start.1 = (bf16[256,2048]{1,0:T(8,128)(2,1)S(1)}, bf16[256,2048]{1,0:T(8,128)(2,1)}, u32[]{:S(2)}) copy-start(bf16[256,2048]{1,0:T(8,128)(2,1)} %w_ref.1) | copy-start | bytes 3145732
  3.3 1.0 copy-start.2
  4.3 1.0 copy-start.3
  5.3 0.7 copy-start.4
  5.9 0.7 copy-start.5

commit v3 on v2

--- a/solution.py
+++ b/solution.py
@@ -187,15 +187,23 @@
 
     tile = min(nh, 512)
 
-    def project(d, t):
+    def project(d, t, parts=1, part=0):
         off = pl.multiple_of(chip_of(d, t) * (CORES * kd), CORES * kd)
         x_part = x_all[:, :, pl.ds(off, CORES * kd)].reshape(n_out * rows, CORES * kd)
+        take = kd // parts
         for j in range(nh // tile):
-            lo = d * nh + j * tile
-            acc[:, lo : lo + tile] += jnp.dot(
-                x_part, wbuf[d, t, :, j * tile : (j + 1) * tile],
-                preferred_element_type=F32,
-            )
+            lo, cols = d * nh + j * tile, slice(j * tile, (j + 1) * tile)
+            if parts == 1:
+                more = jnp.dot(x_part, wbuf[d, t, :, cols], preferred_element_type=F32)
+            else:
+                more = 0.0
+                for c in range(CORES):
+                    at = c * kd + part * take
+                    more += jnp.dot(
+                        x_part[:, at : at + take], wbuf[d, t, at : at + take, cols],
+                        preferred_element_type=F32,
+                    )
+            acc[:, lo : lo + tile] += more
 
     def update(d, t):
         for c in range(CORES):
@@ -234,29 +242,43 @@
             block_to(k).wait_recv()
 
     todo = []
+    halves = 2 if kd % 256 == 0 and pieces % 2 == 0 else 1
     ready = max(1, n_chip // 2)
+    last = n_chip - 1
     for t in range(n_chip):
         if t == ready:
             todo = [start_rows, start_update] + todo
-        for s in order:
+        for n, s in enumerate(order):
             for d in range(2):
                 if t:
                     ring(d, t - 1, s).wait_recv()
-                    if t < n_chip - 1:
+                    if t < last:
                         ring(d, t, s).start()
                     across(d, t, s, core).start()
-            if t >= ready and t < n_chip - 1:
+            if t >= ready:
                 for _ in range(min(3, len(todo))):
                     todo.pop(0)()
-        for s in order:
-            for d in range(2):
-                across(d, t, s, 1 - core).wait_recv()
-        for d in range(2):
-            todo.append(functools.partial(update, d, t))
-            todo.append(functools.partial(project, d, t))
-    for job in todo:
-        job()
-
+            if t == last and n:
+                before = order[n - 1]
+                for d in range(2):
+                    across(d, t, before, 1 - core).wait_recv()
+                if before == pieces:
+                    for d in range(2):
+                        update(d, t)
+                elif halves == 2 and before == pieces // 2 - 1:
+                    for d in range(2):
+                        project(d, t, 2, 0)
+        if t == last:
+            for d in range(2):
+                across(d, t, order[-1], 1 - core).wait_recv()
+                project(d, t, halves, halves - 1)
+        else:
+            for s in order:
+                for d in range(2):
+                    across(d, t, s, 1 - core).wait_recv()
+            for d in range(2):
+                todo.append(functools.partial(update, d, t))
+                todo.append(functools.partial(project, d, t))
 
     for t in range(n_chip):
         for s in order:
@@ -315,7 +337,7 @@
                 dma((7,)),
             ],
             compiler_params=pltpu.CompilerParams(
-                collective_id=0, has_side_effects=True, vmem_limit_bytes=44 * 2**20
+                collective_id=0, has_side_effects=True, vmem_limit_bytes=60 * 2**20
             ),
         )(
             inputs,

time: 115 us -> 111 us (0.965)
  local copies, waits for them, and re-layouts: 5.93 us -> 0.01 us
  other arithmetic: 2.87 us -> 4.92 us
    unnamed x12 -> x2, local copies, waits for them, and re-layouts: 5.93 us -> 0.01 us
    convert_element_type x1, other arithmetic: 1.36 us -> 3.41 us  [step(): return (total.astype(BF16), update_sum * scale)]
where the time goes in v3:
time: 111 us; the launch traced here: 110 us
  Pallas kernels  105 us (95%)
  other arithmetic  4.92 us (4%)
    pallas_call x1, Pallas kernels, step(): pl.pallas_call(functools.partial(kernel, n_pop, n_out, pieces), out_shape...  105 us
    convert_element_type x1, other arithmetic, step(): return (total.astype(BF16), update_sum * scale)  3.41 us

profile of v3, /device:TPU:0, one launch (start us, length us, event | category | flops | bytes accessed | tf_op | source)
XLA Modules:
  0.0 110.4 jit_solution(2666107481379737298)
XLA Ops:
  0.6 104.9 %shard_map.77 = (f32[384,2048]{1,0:T(8,128)}, f32[256,2048]{1,0:T(8,128)}) custom-call(bf16[192,4096]{1,0:T(8,128)(2,1)} %x_ref.1, bf16[256,2048]{1,0:T(8,128)(2,1)} %w_ref.1, bf16[48,4096]{1,0:T(8,128)(2,1)} %a_ref.1, bf16[2,48,2048]{2,1,0:T(8,128)(2,1)} %bitcast.3, f32[1,96]{1,0:T(1,128)} %bitcast.4, s32[1,24]{1,0:T(1,128)} %bitcast.5), custom_call_target="tpu_custom_call" | custom-call | tf_op jit(solution)/shard_map/pallas_call | solution.py:309
  105.5 0.0 copy-start
  105.5 3.4 %convert_element_type.3 = bf16[384,2048]{1,0:T(8,128)(2,1)} convert(f32[384,2048]{1,0:T(8,128)} %get-tuple-element.4) | non-fusion elementwise | flops 786432 | bytes 4718592 | tf_op jit(solution)/shard_map/convert_element_type | solution.py:350
  108.9 0.0 copy-done
  108.9 1.5 %broadcast_multiply_fusion = f32[256,2048]{1,0:T(8,128)} fusion(f32[256,2048]{1,0:T(8,128)S(1)} %copy-done), kind=kLoop, calls=%fused_computation | loop fusion | flops 524288 | bytes 4194304 | tf_op jit(solution)/shard_map/mul | solution.py:350
Async XLA Ops:
  105.5 3.4 %copy-start = (f32[256,2048]{1,0:T(8,128)S(1)}, f32[256,2048]{1,0:T(8,128)}, u32[]{:S(2)}) copy-start(f32[256,2048]{1,0:T(8,128)} %get-tuple-element.5) | copy-start | bytes 6291460

commit v4 on v3

--- a/solution.py
+++ b/solution.py
@@ -21,10 +21,10 @@
 
 
 def kernel(
-    n_pop, n_out, pieces,
+    n_pop, n_out, pieces, scale,
     x_ref, w_ref, a_ref, b_hbm, f_hbm, e_hbm,
-    acc, upd_ref,
-    wbuf, bbuf, x_all, a_all, s_src, s_all, b_ref, f_ref, e_ref,
+    out_ref, upd_hbm,
+    acc, upd_ref, wbuf, bbuf, x_all, a_all, s_src, s_all, b_ref, f_ref, e_ref,
     ring_send, ring_recv, pair_send, pair_recv,
     xs_send, xs_recv, as_send, as_recv, s_send, s_recv, loc_sem,
 ):
@@ -245,6 +245,7 @@
     halves = 2 if kd % 256 == 0 and pieces % 2 == 0 else 1
     ready = max(1, n_chip // 2)
     last = n_chip - 1
+    upd_out = pltpu.make_async_copy(upd_ref, upd_hbm, loc_sem.at[7])
     for t in range(n_chip):
         if t == ready:
             todo = [start_rows, start_update] + todo
@@ -256,7 +257,7 @@
                         ring(d, t, s).start()
                     across(d, t, s, core).start()
             if t >= ready:
-                for _ in range(min(3, len(todo))):
+                for _ in range(min(2, len(todo))):
                     todo.pop(0)()
             if t == last and n:
                 before = order[n - 1]
@@ -265,6 +266,8 @@
                 if before == pieces:
                     for d in range(2):
                         update(d, t)
+                    upd_ref[...] = upd_ref[...] * scale
+                    upd_out.start()
                 elif halves == 2 and before == pieces // 2 - 1:
                     for d in range(2):
                         project(d, t, 2, 0)
@@ -272,6 +275,9 @@
             for d in range(2):
                 across(d, t, order[-1], 1 - core).wait_recv()
                 project(d, t, halves, halves - 1)
+                cols = slice(d * nh, (d + 1) * nh)
+                out_ref[:, cols] = acc[:, cols].astype(BF16)
+            upd_out.wait()
         else:
             for s in order:
                 for d in range(2):
@@ -293,6 +299,24 @@
         block_to(k).wait_send()
 
 
+def hand_on(cuts, total_ref, sum_ref, out_ref, upd_ref, total, update, in_sem, out_sem):
+    arrays = ((total_ref, total, out_ref), (sum_ref, update, upd_ref))
+    into, out = [], []
+    for cut in range(cuts):
+        for k, (src, mid, dst) in enumerate(arrays):
+            size = src.shape[0] // cuts
+            at = pl.ds(cut * size, size)
+            into.append(pltpu.make_async_copy(src.at[at], mid.at[at], in_sem.at[k, cut]))
+            out.append(pltpu.make_async_copy(mid.at[at], dst.at[at], out_sem.at[k, cut]))
+    for copy in into:
+        copy.start()
+    for arrived, copy in zip(into, out):
+        arrived.wait()
+        copy.start()
+    for copy in out:
+        copy.wait()
+
+
 def solution(mesh):
     n_pop, n_out = mesh.shape["pop"], mesh.shape["out"]
     n_chip = n_pop // CORES
@@ -302,19 +326,21 @@
         kd, n_cols = projection.shape
         members, elite = factor_a.shape[0], elite_idx.shape[0]
         nh = n_cols // 2
-        pieces = min(4, kd // 16)
+        pieces = min(8, kd // 16)
         scale = math.sqrt(d_in / (n_pop * elite))
         dma = pltpu.SemaphoreType.DMA
         hbm, vmem = pl.BlockSpec(memory_space=pltpu.HBM), pl.BlockSpec(memory_space=pltpu.VMEM)
         total, update_sum = pl.pallas_call(
-            functools.partial(kernel, n_pop, n_out, pieces),
+            functools.partial(kernel, n_pop, n_out, pieces, scale),
             out_shape=(
-                jax.ShapeDtypeStruct((n_out * rows, n_cols), F32),
+                jax.ShapeDtypeStruct((n_out * rows, n_cols), BF16),
                 jax.ShapeDtypeStruct((kd, n_cols), F32),
             ),
             in_specs=[hbm] * 6,
-            out_specs=(vmem, vmem),
+            out_specs=(vmem, pl.BlockSpec(memory_space=pl.ANY)),
             scratch_shapes=[
+                pltpu.VMEM((n_out * rows, n_cols), F32),
+                pltpu.VMEM((kd, n_cols), F32),
                 pltpu.VMEM((2, n_chip, CORES * kd, nh), BF16),
                 pltpu.VMEM((2, n_chip, CORES, elite, nh), BF16),
                 pltpu.VMEM((n_out, rows, d_in), BF16),
@@ -334,7 +360,7 @@
                 dma((n_out,)),
                 dma((n_pop,)),
                 dma((n_pop,)),
-                dma((7,)),
+                dma((8,)),
             ],
             compiler_params=pltpu.CompilerParams(
                 collective_id=0, has_side_effects=True, vmem_limit_bytes=60 * 2**20
@@ -347,7 +373,22 @@
             fitness_w.reshape(1, -1),
             elite_idx.reshape(1, -1),
         )
-        return total.astype(BF16), update_sum * scale
+        cuts = 4
+        return pl.pallas_call(
+            functools.partial(hand_on, cuts),
+            out_shape=(
+                jax.ShapeDtypeStruct(total.shape, BF16),
+                jax.ShapeDtypeStruct(update_sum.shape, F32),
+            ),
+            in_specs=[pl.BlockSpec(memory_space=pl.ANY)] * 2,
+            out_specs=(pl.BlockSpec(memory_space=pl.ANY),) * 2,
+            scratch_shapes=[
+                pltpu.VMEM(total.shape, BF16),
+                pltpu.VMEM(update_sum.shape, F32),
+                dma((2, cuts)),
+                dma((2, cuts)),
+            ],
+        )(total, update_sum)
 
     return jax.shard_map(
         step,

time: 111 us -> 111 us (level)
  Pallas kernels: 105 us -> 110 us
  other arithmetic: 4.92 us -> 0 us
    pallas_call x1 -> x2, Pallas kernels: 105 us -> 110 us  [the longest x1 106 us: step(): pl.pallas_call(functools.partial(kernel, n_pop, n_out, pieces, scale), ou...]
    convert_element_type x1 -> x0, other arithmetic: 3.41 us -> none  [step(): return (total.astype(BF16), update_sum * scale)]
    mul x1 -> x0, other arithmetic: 1.5 us -> none  [step(): return (total.astype(BF16), update_sum * scale)]
where the time goes in v4:
time: 111 us; the launch traced here: 110 us
  Pallas kernels  110 us (99%)
    pallas_call x1, Pallas kernels, step(): pl.pallas_call(functools.partial(kernel, n_pop, n_out, pieces, scale), ou...  106 us
    pallas_call x1, Pallas kernels, step(): pl.pallas_call(functools.partial(hand_on, cuts), out_shape=(jax.ShapeDtyp...  3.16 us

profile of v4, /device:TPU:0, one launch (start us, length us, event | category | flops | bytes accessed | tf_op | source)
XLA Modules:
  0.0 110.4 jit_solution(3556108606331352470)
XLA Ops:
  0.6 106.4 %shard_map.77 = (bf16[384,2048]{1,0:T(8,128)(2,1)}, f32[256,2048]{1,0:T(8,128)}) custom-call(bf16[192,4096]{1,0:T(8,128)(2,1)} %x_ref.1, bf16[256,2048]{1,0:T(8,128)(2,1)} %w_ref.1, bf16[48,4096]{1,0:T(8,128)(2,1)} %a_ref.1, bf16[2,48,2048]{2,1,0:T(8,128)(2,1)} %bitcast.3, f32[1,96]{1,0:T(1,128)} %bitcast.4, s32[1,24]{1,0:T(1,128)} %bitcast.5), custom_call_target="tpu_custom_call" | custom-call | tf_op jit(solution)/shard_map/pallas_call | solution.py:333
  107.0 3.2 %shard_map.78 = (bf16[384,2048]{1,0:T(8,128)(2,1)}, f32[256,2048]{1,0:T(8,128)}) custom-call(bf16[384,2048]{1,0:T(8,128)(2,1)} %get-tuple-element.4.total_ref, f32[256,2048]{1,0:T(8,128)} %get-tuple-element.5.sum_ref), custom_call_target="tpu_custom_call" | custom-call | tf_op jit(solution)/shard_map/pallas_call | solution.py:377

commit v5 on v4

--- a/solution.py
+++ b/solution.py
@@ -257,7 +257,7 @@
                         ring(d, t, s).start()
                     across(d, t, s, core).start()
             if t >= ready:
-                for _ in range(min(2, len(todo))):
+                for _ in range(min(3, len(todo))):
                     todo.pop(0)()
             if t == last and n:
                 before = order[n - 1]
@@ -326,7 +326,7 @@
         kd, n_cols = projection.shape
         members, elite = factor_a.shape[0], elite_idx.shape[0]
         nh = n_cols // 2
-        pieces = min(8, kd // 16)
+        pieces = min(4, kd // 16)
         scale = math.sqrt(d_in / (n_pop * elite))
         dma = pltpu.SemaphoreType.DMA
         hbm, vmem = pl.BlockSpec(memory_space=pltpu.HBM), pl.BlockSpec(memory_space=pltpu.VMEM)

time: 111 us -> 108 us (0.973)
  Pallas kernels: 110 us -> 107 us
    pallas_call x1, Pallas kernels: 106 us -> 104 us  [step(): pl.pallas_call(functools.partial(kernel, n_pop, n_out, pieces, scale), ou...]
where the time goes in v5:
time: 108 us
  Pallas kernels  107 us (99%)
    pallas_call x1, Pallas kernels, step(): pl.pallas_call(functools.partial(kernel, n_pop, n_out, pieces, scale), ou...  104 us
    pallas_call x1, Pallas kernels, step(): pl.pallas_call(functools.partial(hand_on, cuts), out_shape=(jax.ShapeDtyp...  3.16 us

profile of v5, /device:TPU:0, one launch (start us, length us, event | category | flops | bytes accessed | tf_op | source)
XLA Modules:
  0.0 107.9 jit_solution(17952503104635002871)
XLA Ops:
  0.6 103.9 %shard_map.77 = (bf16[384,2048]{1,0:T(8,128)(2,1)}, f32[256,2048]{1,0:T(8,128)}) custom-call(bf16[192,4096]{1,0:T(8,128)(2,1)} %x_ref.1, bf16[256,2048]{1,0:T(8,128)(2,1)} %w_ref.1, bf16[48,4096]{1,0:T(8,128)(2,1)} %a_ref.1, bf16[2,48,2048]{2,1,0:T(8,128)(2,1)} %bitcast.3, f32[1,96]{1,0:T(1,128)} %bitcast.4, s32[1,24]{1,0:T(1,128)} %bitcast.5), custom_call_target="tpu_custom_call" | custom-call | tf_op jit(solution)/shard_map/pallas_call | solution.py:333
  104.6 3.2 %shard_map.78 = (bf16[384,2048]{1,0:T(8,128)(2,1)}, f32[256,2048]{1,0:T(8,128)}) custom-call(bf16[384,2048]{1,0:T(8,128)(2,1)} %get-tuple-element.4.total_ref, f32[256,2048]{1,0:T(8,128)} %get-tuple-element.5.sum_ref), custom_call_target="tpu_custom_call" | custom-call | tf_op jit(solution)/shard_map/pallas_call | solution.py:377
